TPU v7x, 32 devices: a whole 2x2x4 slice. The times are simulated.
32 devices in a mesh: groups: 1, mode: 32 (over z, y, x, core).
Axes of the slice: x: 2, y: 2, z: 4, core: 2. Of those that a mesh axis runs over, the one named last changes fastest.
Arguments:
- basis: bfloat16 [384, 16384], P('groups', 'mode')
- slab_region: int32 [128], P(('groups', 'mode')), may hold values from 0 to 8
- coef_index: int32 [9, 6], P('groups'), may hold values from 0 to 8
- coef_table: float32 [8], P('groups'), may hold values from 0.2 to 5
Outputs:
- gram: float32 [21, 384, 384], P(None, ('groups', 'mode'))
All inputs are finite; a program needn't handle non-finite values.
Results may differ from a plain program's by a relative error of at most 0.0005.
The roundings to bfloat16 on the way count: a program that leaves them out, or rounds other values in their place, can miss the bound.
Values may be sent and summed in bfloat16 or wider, within the bound.
A program may use at most 128 MiB of HBM per device.

v0:
```python
import jax
import jax.numpy as jnp
from jax import lax
from jax.sharding import PartitionSpec as P


def extended(block, sides, width):
    for axis, dim in sides:
        count = lax.axis_size(axis)
        forward = [(i, i + 1) for i in range(count - 1)]
        forward.append((count - 1, 0))
        backward = [(target, source) for source, target in forward]
        low = lax.ppermute(
            lax.slice_in_dim(block, block.shape[dim] - width, None, axis=dim), axis, forward
        )
        high = lax.ppermute(lax.slice_in_dim(block, 0, width, axis=dim), axis, backward)
        block = jnp.concatenate([low, block, high], axis=dim)
    return block


def slab_weights(slab_region, coef_index, coef_table):
    regions = coef_index.shape[0]
    entries = coef_table.shape[0]
    table_hit = (
        coef_index[:, :, None] == jnp.arange(entries, dtype=jnp.int32)[None, None, :]
    ).astype(jnp.float32)
    kappa = jnp.sum(table_hit * coef_table[None, None, :], axis=2)
    region_hit = (slab_region[:, None] == jnp.arange(regions, dtype=jnp.int32)[None, :]).astype(
        jnp.float32
    )
    return jnp.sum(region_hit[:, :, None] * kappa[None, :, :], axis=1)


def term_actions(padded, slab_kappa):
    rows = padded.shape[0]
    slabs = padded.shape[1] - 2
    width = padded.shape[2]
    terms = slab_kappa.shape[1]
    field = padded[:, 1:-1, :].astype(jnp.float32)
    prev_s = padded[:, :-2, :].astype(jnp.float32)
    next_s = padded[:, 2:, :].astype(jnp.float32)
    zero_col = jnp.zeros((rows, slabs, 1), jnp.float32)
    left_w = jnp.concatenate([zero_col, field[:, :, :-1]], axis=2)
    right_w = jnp.concatenate([field[:, :, 1:], zero_col], axis=2)
    mirror = field[:, :, ::-1]
    stencils = [
        2.0 * field - prev_s - next_s,
        2.0 * field - left_w - right_w,
        field - prev_s,
        field - next_s,
        field - mirror,
        field,
    ]
    result = [
        (slab_kappa[None, :, term, None] * stencils[term])
        .reshape(rows, slabs * width)
        .astype(jnp.bfloat16)
        for term in range(terms)
    ]
    return jnp.stack(result, axis=0)


def per_device(basis, slab_region, coef_index, coef_table):
    terms = coef_index.shape[1]
    rows, cells_dev = basis.shape
    slabs_dev = slab_region.shape[0]
    width = cells_dev // slabs_dev
    devices = lax.axis_size("mode")
    total_cells = cells_dev * devices
    slab_kappa = slab_weights(slab_region, coef_index, coef_table)
    field = basis.reshape(rows, slabs_dev, width)
    padded = extended(field, (("mode", 1),), 1)
    actions = term_actions(padded, slab_kappa)
    pair_list = [(first, second) for first in range(terms) for second in range(first, terms)]
    values = actions.astype(jnp.float32)
    level_sums = lax.psum(jnp.sum(values * values, axis=(1, 2)), "mode")
    pieces = []
    for partial_first in range(terms):
        others = actions[partial_first:].reshape((terms - partial_first) * rows, cells_dev)
        pieces.append(
            lax.dot_general(
                actions[partial_first],
                others,
                (((1,), (1,)), ((), ())),
                preferred_element_type=jnp.float32,
            )
        )
    raw = lax.psum_scatter(
        jnp.concatenate(pieces, axis=1).reshape(rows, len(pair_list), rows),
        "mode",
        scatter_dimension=0,
        tiled=True,
    )
    level = level_sums / (rows * total_cells) + 1e-06
    factors = jnp.stack(
        [
            1.0 / (total_cells * jnp.sqrt(level[first] * level[second]))
            for first, second in pair_list
        ]
    )
    return jnp.transpose(raw * factors[None, :, None], (1, 0, 2))


def solution(mesh):
    return jax.shard_map(
        per_device,
        mesh=mesh,
        in_specs=(P("groups", "mode"), P(("groups", "mode")), P("groups", None), P("groups")),
        out_specs=P(None, ("groups", "mode"), None),
        check_vma=False,
    )
```

profile of v0, /device:TPU:0, one launch (start us, length us, event | category | flops | bytes accessed | tf_op | source)
XLA Modules:
  0.0 243.5 jit_solution(2782310361562966436)
XLA Ops:
  6.5 0.0 reduce-scatter.2.cloned.1.call-start
  6.5 1.1 reshape.267
  7.7 0.3 fusion.20
  8.0 0.5 collective-permute-start
  8.5 6.0 %collective-permute-start.1 = (bf16[384,1,128]{2,1,0:T(2,128)(2,1)S(1)}, bf16[384,1,128]{2,1,0:T(2,128)(2,1)S(1)}, u32[]{:S(2)}, u32[]{:S(2)}) collective-permute-start(bf16[384,1,128]{2,1,0:T(2,128)(2,1)S(1)} %get-tuple-element.23), channel_id=1, source_target_pairs={{1,0},{2,1},{3,2},{4,3},{5,4},{6,5},{7,6},{8,7},{9,8},{10,9},{11,1... | collective-permute-start | bytes 294920 | tf_op jit(solution)/shard_map/ppermute | solution.py:16
  14.5 1.2 fusion.19
  15.7 0.1 fusion.17
  15.7 0.1 select_reduce_fusion
  15.8 0.1 multiply_reduce_fusion.1
  15.9 0.6 slice_bitcast_fusion
  16.5 0.1 broadcast_bitcast_fusion
  16.6 0.9 rev.3
  17.5 0.4 collective-permute-done
  17.9 0.0 collective-permute-done.1
  17.9 3.9 %fusion.5 = (bf16[384,4,128]{2,1,0:T(4,128)(2,1)S(1)}, bf16[384,4,128]{2,1,0:T(4,128)(2,1)S(1)}, bf16[384,4,128]{2,1,0:T(4,128)(2,1)S(1)}, bf16[384,4,128]{2,1,0:T(4,128)(2,1)}, bf16[384,4,128]{2,1,0:T(4,128)(2,1)}) fusion(bf16[384,4,128]{2,1,0:T(4,128)(2,1)S(1)} %reshape.267, bf16[384,1,128]{2,1,0:T(2,128)(2,1)S(1)} %collective-permute-done.1, ...), kind=kLoop, calls=%fused_computation.18 | loop fusion | flops 5308416 | bytes 4902992 | tf_op jit(solution)/shard_map/convert_element_type | solution.py:57
  21.8 1.0 convert_element_type.112
  22.8 1.0 constant_dynamic-update-slice_fusion.5
  23.8 1.9 convert_element_type.114
  25.7 0.9 convert_element_type.116
  26.6 0.2 convert_element_type.118
  26.8 1.1 convert_element_type.120
  27.9 0.0 copy-start.7
  27.9 1.1 constant_dynamic-update-slice_fusion.10
  29.1 0.0 copy-start.5
  29.1 1.1 constant_dynamic-update-slice_fusion.9
  30.2 0.1 constant_dynamic-update-slice_fusion.8
  30.2 0.1 constant_dynamic-update-slice_fusion.7
  30.3 0.1 constant_dynamic-update-slice_fusion.6
  30.4 0.2 pad_maximum_fusion
  30.6 0.1 pad_maximum_fusion.1
  30.8 0.1 pad_maximum_fusion.2
  30.9 0.0 copy-start.6
  30.9 2.9 %convolution_dynamic-update-slice_fusion = f32[384,8064]{1,0:T(8,128)} fusion(bf16[2304,512]{1,0:T(8,128)(2,1)S(1)} %bitcast.51, bf16[48,8,4,128]{3,2,1,0:T(4,128)(2,1)S(1)} %bitcast.54), kind=kOutput, calls=%fused_computation | convolution fusion | flops 905969664 | bytes 6291456 | tf_op jit(solution)/shard_map/dot_general | solution.py:81
  33.8 2.6 %convolution_dynamic-update-slice_fusion.2 = f32[384,8064]{1,0:T(8,128)} fusion(f32[384,8064]{1,0:T(8,128)} %convolution_dynamic-update-slice_fusion, bf16[1920,512]{1,0:T(8,128)(2,1)S(1)} %bitcast.60, bf16[48,8,4,128]{3,2,1,0:T(4,128)(2,1)S(1)} %bitcast.58), kind=kOutput, calls=%fused_computation.3 | convolution fusion | flops 754974720 | bytes 5308416 | tf_op jit(solution)/shard_map/dot_general | solution.py:81
  36.4 0.0 copy-done.4
  36.4 2.2 convolution_dynamic-update-slice_fusion.1
  38.7 2.0 convolution_dynamic-update-slice_fusion.3
  40.7 1.6 convolution_dynamic-update-slice_fusion.4
  42.2 1.3 convolution_dynamic-update-slice_fusion.5
  43.5 12.6 %copy.16 = f32[384,8064]{0,1:T(8,128)} copy(f32[384,8064]{1,0:T(8,128)} %convolution_dynamic-update-slice_fusion.5) | data formatting | bytes 24772608 | tf_op jit(solution)/shard_map/concatenate | solution.py:89
  56.1 14.8 %copy.17 = f32[384,21,384]{2,1,0:T(8,128)} copy(f32[384,21,384]{0,2,1:T(8,128)} %bitcast.50) | data formatting | bytes 24772608 | tf_op jit(solution)/shard_map/reshape | solution.py:89
  70.9 0.0 reduce-scatter.2.cloned.1.call-update
  70.9 0.6 multiply_reduce_fusion
  71.6 38.6 %psum.7 = f32[6]{0:T(128)S(1)} all-reduce(f32[6]{0:T(128)S(1)} %multiply_reduce_fusion), channel_id=1, replica_groups=mesh['groups'=1,'mode'=32] {'mode'}, use_global_device_ids=true, to_apply=%region_4.0 | all-reduce | flops 6 | bytes 48 | tf_op jit(solution)/shard_map/psum | solution.py:76
  110.2 0.7 fusion.21
  139.4 0.1 stack.20
  139.5 95.3 %reduce-scatter.2.cloned.1.call-done = f32[12,21,384]{2,1,0:T(8,128)} async-done(((f32[384,21,384]{2,1,0:T(8,128)}), f32[12,21,384]{2,1,0:T(8,128)}) %reduce-scatter.2.cloned.1.call-update) | async-done | bytes 387088 | tf_op jit(solution)/shard_map/reduce_scatter | solution.py:88
  234.8 1.9 multiply_bitcast_fusion
  (20 shorter events, 0.1 us)
Async XLA Ops:
  6.5 9.1 %copy-start.9 = (s32[4]{0:T(128)S(1)}, s32[4]{0:T(128)}, u32[]{:S(2)}) copy-start(s32[4]{0:T(128)} %param.5) | copy-start | bytes 52
  6.5 9.2 %copy-start.8 = (s32[9,6]{0,1:T(8,128)S(1)}, s32[9,6]{0,1:T(8,128)}, u32[]{:S(2)}) copy-start(s32[9,6]{0,1:T(8,128)} %param.6) | copy-start | bytes 652
  6.5 9.2 %copy-start.10 = (f32[8]{0:T(128)S(1)}, f32[8]{0:T(128)}, u32[]{:S(2)}) copy-start(f32[8]{0:T(128)} %param.7) | copy-start | bytes 100
  6.5 228.2 %reduce-scatter.2.cloned.1.call-start = ((), (), s32[]{:S(2)}) async-start(), calls=%async_computation.1 | async-start | bytes 14598144 | tf_op jit(solution)/shard_map/reduce_scatter | solution.py:88
  8.0 9.9 %collective-permute-start = (bf16[384,1,128]{2,1,0:T(2,128)(2,1)S(1)}, bf16[384,1,128]{2,1,0:T(2,128)(2,1)S(1)}, u32[]{:S(2)}, u32[]{:S(2)}) collective-permute-start(bf16[384,1,128]{2,1,0:T(2,128)(2,1)S(1)} %get-tuple-element.22), channel_id=1, source_target_pairs={{0,1},{1,2},{2,3},{3,4},{4,5},{5,6},{6,7},{7,8},{8,9},{9,10},{10,1... | collective-permute-start | bytes 294920 | tf_op jit(solution)/shard_map/ppermute | solution.py:13
  8.5 9.4 %collective-permute-start.1 = (bf16[384,1,128]{2,1,0:T(2,128)(2,1)S(1)}, bf16[384,1,128]{2,1,0:T(2,128)(2,1)S(1)}, u32[]{:S(2)}, u32[]{:S(2)}) collective-permute-start(bf16[384,1,128]{2,1,0:T(2,128)(2,1)S(1)} %get-tuple-element.23), channel_id=1, source_target_pairs={{1,0},{2,1},{3,2},{4,3},{5,4},{6,5},{7,6},{8,7},{9,8},{10,9},{11,1... | collective-permute-start | bytes 294920 | tf_op jit(solution)/shard_map/ppermute | solution.py:16
  21.8 4.9 %copy-start.3 = (bf16[384,4,128]{2,1,0:T(4,128)(2,1)}, bf16[384,4,128]{2,1,0:T(4,128)(2,1)S(1)}, u32[]{:S(2)}) copy-start(bf16[384,4,128]{2,1,0:T(4,128)(2,1)S(1)} %get-tuple-element.9) | copy-start | bytes 1179652
  21.8 5.0 %copy-start.1 = (bf16[384,4,128]{2,1,0:T(4,128)(2,1)}, bf16[384,4,128]{2,1,0:T(4,128)(2,1)S(1)}, u32[]{:S(2)}) copy-start(bf16[384,4,128]{2,1,0:T(4,128)(2,1)S(1)} %get-tuple-element.7) | copy-start | bytes 1179652
  27.9 2.4 copy-start.7
  29.1 1.4 copy-start.5
  30.9 2.9 %copy-start.6 = (bf16[384,4,128]{2,1,0:T(4,128)(2,1)S(1)}, bf16[384,4,128]{2,1,0:T(4,128)(2,1)}, u32[]{:S(2)}) copy-start(bf16[384,4,128]{2,1,0:T(4,128)(2,1)} %get-tuple-element.19) | copy-start | bytes 1179652
  33.8 2.6 %copy-start.4 = (bf16[384,4,128]{2,1,0:T(4,128)(2,1)S(1)}, bf16[384,4,128]{2,1,0:T(4,128)(2,1)}, u32[]{:S(2)}) copy-start(bf16[384,4,128]{2,1,0:T(4,128)(2,1)} %copy-done.3) | copy-start | bytes 1179652
  36.4 2.2 copy-start.2
  38.7 2.0 copy-start
Sparse Core Ops, SparseCore 0:
  71.1 163.6 reduce-scatter.1
where the time goes:
time: 245 us; the launch traced here: 243 us
  waiting for transfers between devices  95.7 us (39%)
  between operations  42.1 us (17%)
  local copies, waits for them, and re-layouts  40.8 us (17%)
  blocking collectives  38.6 us (16%)
  matrix products  12.6 us (5%)
  other arithmetic  7.13 us (3%)
  starting transfers between devices  6.52 us (3%)
    reduce_scatter x1, waiting for transfers between devices, per_device(): lax.psum_scatter(jnp.concatenate(pieces, axis=1).reshape(rows, len(pair_l...  95.3 us
    psum x1, blocking collectives, per_device(): level_sums = lax.psum(jnp.sum(values * values, axis=(1, 2)), 'mode')  38.6 us
    reshape x1, local copies, waits for them, and re-layouts, per_device(): jnp.concatenate(pieces, axis=1).reshape(rows, len(pair_list), rows)  14.8 us
    dot_general x6, matrix products, per_device(): lax.dot_general(actions[partial_first], others, (((1,), (1,)), ((), ())),...  12.6 us
    concatenate x1, local copies, waits for them, and re-layouts, per_device(): jnp.concatenate(pieces, axis=1).reshape(rows, len(pair_list), rows)  12.6 us
    ppermute x1, starting transfers between devices, extended(): lax.ppermute(lax.slice_in_dim(block, 0, width, axis=dim), axis, backward)  5.97 us
    convert_element_type x5, local copies, waits for them, and re-layouts, term_actions(): result = [(slab_kappa[None, :, term, None] * stencils[term]).reshape(rows...  5.13 us
  transfers between devices with their start and end apart: 3, of which 2 were waited for; matrix products, arithmetic and copies ran while one was open for 2% of the time, Pallas kernels for 0%

commit v1 on v0

v1 whole, which is shorter than its diff:
```python
import jax
import jax.numpy as jnp
from jax import lax
from jax.sharding import PartitionSpec as P


def plane_size(devices, share):
    size = 1
    while (
        4 * size * size <= 2 * devices
        and devices % (2 * size) == 0
        and 2 * size * share <= 24 << 20
    ):
        size *= 2
    return size


def slab_weights(slab_region, coef_index, coef_table):
    regions = coef_index.shape[0]
    entries = coef_table.shape[0]
    table_hit = (
        coef_index[:, :, None] == jnp.arange(entries, dtype=jnp.int32)[None, None, :]
    ).astype(jnp.float32)
    kappa = jnp.sum(table_hit * coef_table[None, None, :], axis=2)
    region_hit = (slab_region[:, None] == jnp.arange(regions, dtype=jnp.int32)[None, :]).astype(
        jnp.float32
    )
    return jnp.sum(region_hit[:, :, None] * kappa[None, :, :], axis=1)


def term_actions(field, low, high, slab_kappa):
    rows, slabs, width = field.shape
    terms = slab_kappa.shape[1]
    prev_s = jnp.concatenate([low, field[:, :-1]], axis=1).astype(jnp.float32)
    next_s = jnp.concatenate([field[:, 1:], high], axis=1).astype(jnp.float32)
    field = field.astype(jnp.float32)
    zero_col = jnp.zeros((rows, slabs, 1), jnp.float32)
    left_w = jnp.concatenate([zero_col, field[:, :, :-1]], axis=2)
    right_w = jnp.concatenate([field[:, :, 1:], zero_col], axis=2)
    mirror = field[:, :, ::-1]
    stencils = [
        2.0 * field - prev_s - next_s,
        2.0 * field - left_w - right_w,
        field - prev_s,
        field - next_s,
        field - mirror,
        field,
    ]
    return [
        (slab_kappa[None, :, term, None] * stencils[term])
        .reshape(rows, slabs * width)
        .astype(jnp.bfloat16)
        for term in range(terms)
    ]


def per_device(basis, slab_region, coef_index, coef_table):
    terms = coef_index.shape[1]
    rows, cells_dev = basis.shape
    slabs_dev = slab_region.shape[0]
    width = cells_dev // slabs_dev
    devices = lax.axis_size("mode")
    total_cells = cells_dev * devices
    inner = plane_size(devices, 2 * terms * rows * cells_dev)
    outer = devices // inner
    own = rows // devices
    slabs = slabs_dev * inner
    planes = [[a * inner + c for c in range(inner)] for a in range(outer)]
    columns = [[a * inner + c for a in range(outer)] for c in range(inner)]
    tags = jnp.broadcast_to(
        slab_region.astype(jnp.bfloat16)[None, :, None], (16, slabs_dev, width)
    ).reshape(16, cells_dev)
    packed = lax.all_gather(
        jnp.concatenate([basis, tags], axis=0), "mode", axis_index_groups=planes, axis=0
    )
    packed = jnp.transpose(packed, (1, 0, 2)).reshape(rows + 16, slabs, width)
    field = packed[:rows]
    region = packed[rows, :, 0].astype(jnp.int32)
    slab_kappa = slab_weights(region, coef_index, coef_table)
    up = [(i, (i + inner) % devices) for i in range(devices)]
    down = [(target, source) for source, target in up]
    low = lax.ppermute(field[:, -1:], "mode", up)
    high = lax.ppermute(field[:, :1], "mode", down)
    acts = term_actions(field, low, high, slab_kappa)
    column = lax.rem(lax.axis_index("mode"), inner)
    mine = []
    for act in acts:
        view = act.reshape(outer, inner, own, slabs * width)
        mine.append(
            lax.dynamic_index_in_dim(view, column, 1, keepdims=False).reshape(
                outer * own, slabs * width
            )
        )
    pair_list = [(first, second) for first in range(terms) for second in range(first, terms)]
    level_sums = lax.psum(
        jnp.stack([jnp.sum(jnp.square(v.astype(jnp.float32))) for v in mine]), "mode"
    )
    pieces = [
        lax.dot_general(
            mine[first], acts[second], (((1,), (1,)), ((), ())), preferred_element_type=jnp.float32
        )
        for first, second in pair_list
    ]
    raw = lax.psum_scatter(
        jnp.concatenate([p.reshape(outer, own, rows)[:, None] for p in pieces], axis=1),
        "mode",
        scatter_dimension=0,
        axis_index_groups=columns,
        tiled=True,
    )[0]
    level = level_sums / (rows * total_cells) + 1e-06
    factors = jnp.stack(
        [
            1.0 / (total_cells * jnp.sqrt(level[first] * level[second]))
            for first, second in pair_list
        ]
    )
    return raw.reshape(len(pair_list), own, rows) * factors[:, None, None]


def solution(mesh):
    return jax.shard_map(
        per_device,
        mesh=mesh,
        in_specs=(P("groups", "mode"), P(("groups", "mode")), P("groups", None), P("groups")),
        out_specs=P(None, ("groups", "mode"), None),
        check_vma=False,
    )
```

time: 245 us -> 348 us (1.42)
  local copies, waits for them, and re-layouts: 40.8 us -> 164 us
  waiting for transfers between devices: 95.7 us -> 34.8 us
  other arithmetic: 7.13 us -> 45.6 us
    reduce_scatter x1, waiting for transfers between devices: 95.3 us -> 0.02 us  [per_device(): lax.psum_scatter(jnp.concatenate([p.reshape(outer, own, rows)[:, None] fo...]
    convert_element_type x5 -> x16, local copies, waits for them, and re-layouts: 5.13 us -> 95.6 us  [the longest x8 38.3 us: term_actions(): return [(slab_kappa[None, :, term, None] * stencils[term]).reshape(rows,...]
    all_gather x0 -> x1, waiting for transfers between devices: none -> 34.7 us  [per_device(): lax.all_gather(jnp.concatenate([basis, tags], axis=0), 'mode', axis_index...]
    rev x1, local copies, waits for them, and re-layouts: 0.89 us -> 31.4 us  [term_actions(): mirror = field[:, :, ::-1]]
    convert_element_type x1 -> x6, other arithmetic: 3.88 us -> 33.8 us  [the longest x2 20.1 us: term_actions(): return [(slab_kappa[None, :, term, None] * stencils[term]).reshape(rows,...]
    reshape x2 -> x1, local copies, waits for them, and re-layouts: 15.9 us -> 5.14 us  [per_device(): packed = jnp.transpose(packed, (1, 0, 2)).reshape(rows + 16, slabs, width)]
    concatenate x1, local copies, waits for them, and re-layouts: 12.6 us -> 2.13 us  [per_device(): jnp.concatenate([p.reshape(outer, own, rows)[:, None] for p in pieces], a...]
    slice x1 -> x4, local copies, waits for them, and re-layouts: 0.28 us -> 7.95 us  [the longest x1 3.78 us: term_actions(): prev_s = jnp.concatenate([low, field[:, :-1]], axis=1).astype(jnp.float32)]
  transfers between devices with their start and end apart: 3 -> 4, of which waited for: 2 -> 1; matrix products, arithmetic and copies ran while one was open for 2% -> 19% of each run, Pallas kernels for 0% -> 0%
where the time goes in v1:
time: 348 us; the launch traced here: 346 us
  local copies, waits for them, and re-layouts  164 us (47%)
  other arithmetic  45.6 us (13%)
  between operations  43 us (12%)
  blocking collectives  39.4 us (11%)
  waiting for transfers between devices  34.8 us (10%)
  matrix products  15.6 us (4%)
  starting transfers between devices  3.87 us (1%)
    psum x1, blocking collectives, per_device(): lax.psum(jnp.stack([jnp.sum(jnp.square(v.astype(jnp.float32))) for v in m...  39.4 us
    convert_element_type x8, local copies, waits for them, and re-layouts, term_actions(): return [(slab_kappa[None, :, term, None] * stencils[term]).reshape(rows,...  38.3 us
    all_gather x1, waiting for transfers between devices, per_device(): lax.all_gather(jnp.concatenate([basis, tags], axis=0), 'mode', axis_index...  34.7 us
    rev x1, local copies, waits for them, and re-layouts, term_actions(): mirror = field[:, :, ::-1]  31.4 us
    convert_element_type x3, local copies, waits for them, and re-layouts, term_actions(): prev_s = jnp.concatenate([low, field[:, :-1]], axis=1).astype(jnp.float32)  21.4 us
    convert_element_type x3, local copies, waits for them, and re-layouts, term_actions(): next_s = jnp.concatenate([field[:, 1:], high], axis=1).astype(jnp.float32)  21.2 us
    convert_element_type x2, other arithmetic, term_actions(): return [(slab_kappa[None, :, term, None] * stencils[term]).reshape(rows,...  20.1 us
    dot_general x21, matrix products, per_device(): lax.dot_general(mine[first], acts[second], (((1,), (1,)), ((), ())), pref...  15.6 us
  transfers between devices with their start and end apart: 4, of which 1 were waited for; matrix products, arithmetic and copies ran while one was open for 19% of the time, Pallas kernels for 0%

profile of v1, /device:TPU:0, one launch (start us, length us, event | category | flops | bytes accessed | tf_op | source)
XLA Modules:
  0.0 345.8 jit_solution(3930938717261372282)
XLA Ops:
  7.3 1.8 pad_maximum_fusion
  9.1 0.8 select_reduce_fusion
  10.0 34.7 %all-gather.3.cloned.1.call-done = bf16[3200,512]{1,0:T(8,128)(2,1)} async-done(((bf16[400,512]{1,0:T(8,128)(2,1)}), bf16[3200,512]{1,0:T(8,128)(2,1)}) %all-gather.3.cloned.1.call-update) | async-done | bytes 3276816 | tf_op jit(solution)/shard_map/all_gather | solution.py:73
  44.7 6.5 %slice_convert_fusion = (f32[384,8,512]{2,0,1:T(8,128)}, bf16[384,8,512]{2,0,1:T(8,128)(2,1)}) fusion(bf16[400,8,512]{2,0,1:T(8,128)(2,1)} %bitcast.257), kind=kLoop, calls=%fused_computation.133 | loop fusion | flops 1572864 | bytes 12582912 | tf_op jit(solution)/shard_map/convert_element_type | solution.py:36
  51.2 3.4 copy.159
  54.6 3.8 %fusion.69 = (bf16[384,31,128]{0,2,1:T(8,128)(2,1)}, bf16[384,31,128]{0,2,1:T(8,128)(2,1)}) fusion(bf16[384,32,128]{0,2,1:T(8,128)(2,1)S(1)} %bitcast.241), kind=kLoop, calls=%fused_computation.136 | loop fusion | bytes 12189696 | tf_op jit(solution)/shard_map/slice | solution.py:34
  58.4 0.7 fusion.68
  59.1 3.6 %copy.156 = bf16[400,8,512]{2,1,0:T(8,128)(2,1)} copy(bf16[400,8,512]{2,0,1:T(8,128)(2,1)S(1)} %bitcast.258) | data formatting | bytes 6553600 | tf_op jit(solution)/shard_map/transpose | solution.py:76
  62.7 31.4 %rev.3 = f32[384,32,128]{0,2,1:T(8,128)} reverse(bf16[384,32,128]{0,2,1:T(8,128)(2,1)S(1)} %bitcast.243), dimensions={2} | reverse | bytes 9437184 | tf_op jit(solution)/shard_map/rev | solution.py:40
  94.2 5.6 %fusion.67 = (f32[384,32,127]{0,2,1:T(8,128)}, f32[384,32,127]{0,2,1:T(8,128)}) fusion(bf16[384,32,128]{0,2,1:T(8,128)(2,1)S(1)} %bitcast.244), kind=kLoop, calls=%fused_computation.134 | loop fusion | bytes 24969216 | tf_op jit(solution)/shard_map/slice | solution.py:38
  99.8 1.5 collective-permute-start
  101.3 2.3 collective-permute-start.1
  103.6 5.1 %reshape.478 = bf16[400,32,128]{2,1,0:T(8,128)(2,1)S(1)} reshape(bf16[400,8,512]{2,1,0:T(8,128)(2,1)} %copy.156) | data formatting | bytes 6553600 | tf_op jit(solution)/shard_map/reshape | solution.py:76
  109.8 0.7 broadcast_bitcast_fusion
  110.5 10.5 %multiply_convert_fusion = (bf16[384,32,128]{0,2,1:T(8,128)(2,1)S(1)}, bf16[384,32,128]{0,2,1:T(8,128)(2,1)}) fusion(f32[384,32,128]{0,2,1:T(8,128)} %rev.3, f32[32]{0:T(128)S(1)} %get-tuple-element.37, bf16[384,32,128]{0,2,1:T(8,128)(2,1)} %bitcast.245, f32[384,32,127]{0,2,1:T(8,128)} %get-tuple-element.29, f32[384,32,127]{0,2,1:T(8,128)} %get-tuple-element.28, ...), kind=kLoop, calls=%fused_computation.13 | loop fusion | flops 14155776 | bytes 28213504 | tf_op jit(solution)/shard_map/convert_element_type | solution.py:52
  121.0 0.8 broadcast_bitcast_fusion.2
  121.8 6.4 %copy.158 = f32[384,8,512]{2,1,0:T(8,128)} copy(f32[384,8,512]{2,0,1:T(8,128)S(1)} %bitcast.261) | data formatting | bytes 12582912 | tf_op jit(solution)/shard_map/convert_element_type | solution.py:36
  128.2 8.4 %reshape.486 = f32[4,8,12,4096]{3,2,1,0:T(8,128)} reshape(f32[384,8,512]{2,1,0:T(8,128)} %copy.158) | data formatting | bytes 12582912 | tf_op jit(solution)/shard_map/convert_element_type | solution.py:36
  136.6 5.1 %copy.180 = bf16[384,32,128]{2,1,0:T(8,128)(2,1)} copy(bf16[384,32,128]{0,2,1:T(8,128)(2,1)} %get-tuple-element.27) | data formatting | bytes 6291456 | tf_op jit(solution)/shard_map/convert_element_type | solution.py:52
  141.6 6.8 %convert_element_type.216 = bf16[4,8,12,4096]{3,2,1,0:T(8,128)(2,1)} reshape(bf16[384,32,128]{2,1,0:T(8,128)(2,1)} %copy.180) | data formatting | bytes 6291456 | tf_op jit(solution)/shard_map/convert_element_type | solution.py:52
  148.4 3.5 %copy.193 = bf16[384,32,128]{2,1,0:T(8,128)(2,1)} copy(bf16[384,32,128]{0,2,1:T(8,128)(2,1)S(1)} %get-tuple-element.26) | data formatting | bytes 6291456 | tf_op jit(solution)/shard_map/convert_element_type | solution.py:52
  151.9 6.9 %convert_element_type.219 = bf16[4,8,12,4096]{3,2,1,0:T(8,128)(2,1)} reshape(bf16[384,32,128]{2,1,0:T(8,128)(2,1)} %copy.193) | data formatting | bytes 6291456 | tf_op jit(solution)/shard_map/convert_element_type | solution.py:52
  158.8 6.4 %maximum_convert_fusion = (f32[384,32,128]{0,2,1:T(8,128)}, f32[384,32,128]{0,2,1:T(8,128)}) fusion(bf16[384,31,128]{0,2,1:T(8,128)(2,1)S(1)} %copy-done.11, bf16[384,1,128]{0,2,1:T(8,128)(2,1)S(1)} %collective-permute-done, bf16[384,1,128]{0,2,1:T(8,128)(2,1)S(1)} %collective-permute-done.1, bf16[384,31,128]{0,2,1:T(8,128)(2,1)} %get-tuple-element.33), kind=kLoop, calls=%fused_computation.15 | loop fusion | flops 6291456 | bytes 18874368 | tf_op jit(solution)/shard_map/convert_element_type | solution.py:34
  165.2 6.7 %copy.161 = f32[384,32,128]{2,1,0:T(8,128)} copy(f32[384,32,128]{0,2,1:T(8,128)} %get-tuple-element.47) | data formatting | bytes 12582912 | tf_op jit(solution)/shard_map/convert_element_type | solution.py:35
  171.9 6.6 %copy.164 = f32[384,8,512]{2,0,1:T(8,128)} copy(f32[384,8,512]{0,2,1:T(8,128)} %bitcast.256) | data formatting | bytes 12582912 | tf_op jit(solution)/shard_map/convert_element_type | solution.py:35
  178.5 6.7 %copy.160 = f32[384,32,128]{2,1,0:T(8,128)} copy(f32[384,32,128]{0,2,1:T(8,128)} %get-tuple-element.46) | data formatting | bytes 12582912 | tf_op jit(solution)/shard_map/convert_element_type | solution.py:34
  185.2 6.8 %copy.163 = f32[384,8,512]{2,0,1:T(8,128)} copy(f32[384,8,512]{0,2,1:T(8,128)} %bitcast.255) | data formatting | bytes 12582912 | tf_op jit(solution)/shard_map/convert_element_type | solution.py:34
  191.9 9.6 %fusion.7 = (bf16[384,8,512]{2,0,1:T(8,128)(2,1)}, bf16[384,8,512]{2,0,1:T(8,128)(2,1)}, bf16[384,8,512]{2,0,1:T(8,128)(2,1)}, bf16[384,8,512]{2,0,1:T(8,128)(2,1)}) fusion(f32[384,8,512]{2,0,1:T(8,128)} %copy.164, f32[8,512]{1,0:T(8,128)S(1)} %get-tuple-element.53, bf16[400,8,512]{2,0,1:T(8,128)(2,1)S(1)} %bitcast.259, f32[384,8,512]{2,0,1:T(8,128)} %copy.163, ...), kind=kLoop, calls=%fused_computation.11 | loop fusion | flops 22020096 | bytes 28377088 | tf_op jit(solution)/shard_map/convert_element_type | solution.py:52
  201.5 4.6 %copy.165 = bf16[384,8,512]{0,2,1:T(8,128)(2,1)} copy(bf16[384,8,512]{2,0,1:T(8,128)(2,1)} %get-tuple-element.20) | data formatting | bytes 6291456 | tf_op jit(solution)/shard_map/convert_element_type | solution.py:52
  206.2 7.9 %reshape.488 = f32[4,8,12,4096]{3,2,1,0:T(8,128)} reshape(f32[384,32,128]{2,1,0:T(8,128)} %copy.161) | data formatting | bytes 12582912 | tf_op jit(solution)/shard_map/convert_element_type | solution.py:35
  214.1 7.9 %reshape.487 = f32[4,8,12,4096]{3,2,1,0:T(8,128)} reshape(f32[384,32,128]{2,1,0:T(8,128)} %copy.160) | data formatting | bytes 12582912 | tf_op jit(solution)/shard_map/convert_element_type | solution.py:34
  222.1 4.8 %copy.170 = bf16[384,8,512]{0,2,1:T(8,128)(2,1)} copy(bf16[384,8,512]{2,0,1:T(8,128)(2,1)} %get-tuple-element.21) | data formatting | bytes 6291456 | tf_op jit(solution)/shard_map/convert_element_type | solution.py:52
  226.9 2.9 copy.174
  229.8 3.7 %copy.178 = bf16[384,8,512]{0,2,1:T(8,128)(2,1)S(1)} copy(bf16[384,8,512]{2,0,1:T(8,128)(2,1)} %get-tuple-element.23) | data formatting | bytes 6291456 | tf_op jit(solution)/shard_map/convert_element_type | solution.py:52
  233.5 3.4 multiply_reduce_fusion.2
  237.5 1.3 copy-done.5
  240.5 0.9 copy-done.3
  243.8 1.6 copy-done.9
  252.5 1.6 fusion.11
  254.1 1.6 fusion.10
  255.8 1.8 fusion.9
  257.6 2.1 copy.197
  259.8 2.0 multiply_reduce_fusion.4
  261.8 1.9 multiply_reduce_fusion.1
  263.7 3.9 %stack.22 = f32[6]{0:T(128)S(1)} concatenate(f32[1]{0:T(128)} %bitcast.76, f32[1]{0:T(128)} %bitcast.77, f32[1]{0:T(128)} %bitcast.78, f32[1]{0:T(128)} %bitcast.79, f32[1]{0:T(128)} %bitcast.80, f32[1]{0:T(128)} %bitcast.81), dimensions={0} | concatenate | bytes 48 | tf_op jit(solution)/shard_map/stack | solution.py:96
  267.6 39.4 %psum.7 = f32[6]{0:T(128)S(1)} all-reduce(f32[6]{0:T(128)S(1)} %stack.22), channel_id=1, replica_groups=mesh['groups'=1,'mode'=32] {'mode'}, use_global_device_ids=true, to_apply=%region_9.10 | all-reduce | flops 6 | bytes 48 | tf_op jit(solution)/shard_map/psum | solution.py:95
  307.0 0.7 fusion.70
  337.1 1.9 bitcast_multiply_fusion
  (77 shorter events, 13.7 us)
Async XLA Ops:
  6.5 38.2 %all-gather.3.cloned.1.call-start = ((), (), s32[]{:S(2)}) async-start(), calls=%async_computation.2 | async-start | bytes 3686400 | tf_op jit(solution)/shard_map/all_gather | solution.py:73
  9.1 328.0 %reduce-scatter.2.cloned.1.call-start = ((), (), s32[]{:S(2)}) async-start(), calls=%async_computation.1 | async-start | bytes 2211840 | tf_op jit(solution)/shard_map/reduce_scatter | solution.py:104
  54.6 39.6 %copy-start.2 = (bf16[384,8,512]{0,2,1:T(8,128)(2,1)}, bf16[384,8,512]{0,2,1:T(8,128)(2,1)S(1)}, u32[]{:S(2)}) copy-start(bf16[384,8,512]{0,2,1:T(8,128)(2,1)S(1)} %copy.159) | copy-start | bytes 9437188
  54.6 4.5 %copy-start.6 = (bf16[3200,512]{1,0:T(8,128)(2,1)S(1)}, bf16[3200,512]{1,0:T(8,128)(2,1)}, u32[]{:S(2)}) copy-start(bf16[3200,512]{1,0:T(8,128)(2,1)} %all-gather.3.cloned.1.call-done) | copy-start | bytes 9830404
  99.8 59.0 %collective-permute-start = (bf16[384,1,128]{0,2,1:T(8,128)(2,1)}, bf16[384,1,128]{0,2,1:T(8,128)(2,1)S(1)}, u32[]{:S(2)}, u32[]{:S(2)}) collective-permute-start(bf16[384,1,128]{0,2,1:T(8,128)(2,1)} %get-tuple-element.30), channel_id=1, source_target_pairs={{0,8},{1,9},{2,10},{3,11},{4,12},{5,13},{6,14},{7,15},{8,16},{9,17... | collective-permute-start | bytes 294920 | tf_op jit(solution)/shard_map/ppermute | solution.py:82
  101.3 57.5 %collective-permute-start.1 = (bf16[384,1,128]{0,2,1:T(8,128)(2,1)}, bf16[384,1,128]{0,2,1:T(8,128)(2,1)S(1)}, u32[]{:S(2)}, u32[]{:S(2)}) collective-permute-start(bf16[384,1,128]{0,2,1:T(8,128)(2,1)} %get-tuple-element.31), channel_id=1, source_target_pairs={{8,0},{9,1},{10,2},{11,3},{12,4},{13,5},{14,6},{15,7},{16,8},{17,9... | collective-permute-start | bytes 294920 | tf_op jit(solution)/shard_map/ppermute | solution.py:83
  110.5 11.3 %slice-start = ((s8[6291456]{0:T(1024)(128)(4,1)}), s8[4194304]{0:T(1024)(128)(4,1)S(1)}, s32[]{:S(2)}) async-start(s8[6291456]{0:T(1024)(128)(4,1)} %bitcast.260), calls=%async_computation.3 | async-start | bytes 8388608
  110.5 11.3 %slice-start.1 = ((s8[6291456]{0:T(1024)(128)(4,1)}), s8[2097152]{0:T(1024)(128)(4,1)S(1)}, s32[]{:S(2)}) async-start(s8[6291456]{0:T(1024)(128)(4,1)} %bitcast.260), calls=%async_computation.4 | async-start | bytes 4194304
  121.0 27.4 %copy-start = (bf16[384,32,128]{0,2,1:T(8,128)(2,1)}, bf16[384,32,128]{0,2,1:T(8,128)(2,1)S(1)}, u32[]{:S(2)}) copy-start(bf16[384,32,128]{0,2,1:T(8,128)(2,1)S(1)} %get-tuple-element.26) | copy-start | bytes 9437188
  151.9 6.9 %copy-start.11 = (bf16[384,31,128]{0,2,1:T(8,128)(2,1)S(1)}, bf16[384,31,128]{0,2,1:T(8,128)(2,1)}, u32[]{:S(2)}) copy-start(bf16[384,31,128]{0,2,1:T(8,128)(2,1)} %get-tuple-element.32) | copy-start | bytes 9142276
  185.2 6.8 %copy-start.7 = (bf16[3200,512]{1,0:T(8,128)(2,1)S(1)}, bf16[3200,512]{1,0:T(8,128)(2,1)}, u32[]{:S(2)}) copy-start(bf16[3200,512]{1,0:T(8,128)(2,1)} %all-gather.3.cloned.1.call-done) | copy-start | bytes 9830404
  222.1 4.9 %copy-start.10 = (bf16[384,8,512]{2,0,1:T(8,128)(2,1)S(1)}, bf16[384,8,512]{2,0,1:T(8,128)(2,1)}, u32[]{:S(2)}) copy-start(bf16[384,8,512]{2,0,1:T(8,128)(2,1)} %get-tuple-element.19) | copy-start | bytes 9437188
  229.8 3.7 %copy-start.12 = (f32[4096]{0:T(1024)S(1)}, f32[4096]{0:T(1024)}, u32[]{:S(2)}) copy-start(f32[4096]{0:T(1024)} %get-tuple-element.49) | copy-start | bytes 49156
  229.8 3.7 %copy-start.13 = (f32[4096]{0:T(1024)S(1)}, f32[4096]{0:T(1024)}, u32[]{:S(2)}) copy-start(f32[4096]{0:T(1024)} %get-tuple-element.50) | copy-start | bytes 49156
  229.8 3.7 %copy-start.14 = (f32[4096]{0:T(1024)S(1)}, f32[4096]{0:T(1024)}, u32[]{:S(2)}) copy-start(f32[4096]{0:T(1024)} %get-tuple-element.51) | copy-start | bytes 49156
  233.5 3.4 copy-start.8
  236.9 1.9 copy-start.5
  237.5 2.4 copy-start.4
  239.4 2.0 copy-start.3
  240.5 2.1 copy-start.1
  243.2 2.2 copy-start.9
Sparse Core Ops, SparseCore 0:
  9.2 35.4 all-gather.2
  259.9 37.6 reduce-scatter.1

commit v2 on v1

v2 whole, which is shorter than its diff:
```python
import functools

import jax
import jax.numpy as jnp
from jax import lax
from jax.experimental import pallas as pl
from jax.experimental.pallas import tpu as pltpu
from jax.sharding import PartitionSpec as P


def plane_size(devices, share):
    size = 1
    while (
        4 * size * size <= 2 * devices
        and devices % (2 * size) == 0
        and 2 * size * share <= 24 << 20
    ):
        size *= 2
    return size


def slab_weights(slab_region, coef_index, coef_table):
    regions = coef_index.shape[0]
    entries = coef_table.shape[0]
    table_hit = (
        coef_index[:, :, None] == jnp.arange(entries, dtype=jnp.int32)[None, None, :]
    ).astype(jnp.float32)
    kappa = jnp.sum(table_hit * coef_table[None, None, :], axis=2)
    region_hit = (slab_region[:, None] == jnp.arange(regions, dtype=jnp.int32)[None, :]).astype(
        jnp.float32
    )
    return jnp.sum(region_hit[:, :, None] * kappa[None, :, :], axis=1)


def one_action(term, here, before, after, across, opposite, kappa):
    value = here.astype(jnp.float32)
    if term == 0:
        stencil = 2.0 * value - before.astype(jnp.float32) - after.astype(jnp.float32)
    elif term == 1:
        stencil = jnp.dot(here, across, preferred_element_type=jnp.float32)
    elif term == 2:
        stencil = value - before.astype(jnp.float32)
    elif term == 3:
        stencil = value - after.astype(jnp.float32)
    elif term == 4:
        stencil = jnp.dot(here, opposite, preferred_element_type=jnp.float32)
    else:
        stencil = value
    return (kappa * stencil).astype(jnp.bfloat16)


def gram_kernel(terms, inner, outer, own, slabs_dev, total_cells, *refs):
    basis, kap, out = refs[:3]
    field, weights, mine, lhs, act, acc = refs[3:9]
    stages = refs[9 : 9 + terms]
    arrived = refs[9 + terms : 9 + 2 * terms]
    lvl, lvl_col, lvl_mid, lvl_row = refs[9 + 2 * terms : 13 + 2 * terms]
    load_sem, gs, gr, ks, kr, hs, hr, zs, zr, cs, cr, rs, rr = refs[13 + 2 * terms :]
    rows, width = field.shape[1], field.shape[2]
    slabs = inner * slabs_dev
    local = outer * own
    me = lax.axis_index("mode")
    plane = me // inner
    column = me % inner

    def row_peer(d):
        return plane * inner + lax.rem(column + d, inner)

    def col_peer(d):
        return lax.rem(plane + d, outer) * inner + column

    def remote(src, dst, send, recv, peer):
        return pltpu.make_async_remote_copy(
            src_ref=src,
            dst_ref=dst,
            send_sem=send,
            recv_sem=recv,
            device_id={"mode": peer},
            device_id_type=pl.DeviceIdType.MESH,
        )

    loads = []
    for s in range(slabs_dev):
        loads.append(
            pltpu.make_async_copy(
                basis.at[:, pl.ds(s * width, width)],
                field.at[1 + column * slabs_dev + s],
                load_sem.at[s],
            )
        )
    loads.append(
        pltpu.make_async_copy(
            kap, weights.at[pl.ds(column * slabs_dev, slabs_dev)], load_sem.at[slabs_dev]
        )
    )
    for copy in loads:
        copy.start()

    barrier = pltpu.get_barrier_semaphore()
    for d in range(1, inner):
        pl.semaphore_signal(
            barrier, inc=1, device_id={"mode": row_peer(d)}, device_id_type=pl.DeviceIdType.MESH
        )
    for d in range(1, outer):
        pl.semaphore_signal(
            barrier, inc=1, device_id={"mode": col_peer(d)}, device_id_type=pl.DeviceIdType.MESH
        )
    pl.semaphore_wait(barrier, inner + outer - 2)
    for copy in loads:
        copy.wait()

    block = pl.ds(1 + column * slabs_dev, slabs_dev)
    spot = pl.ds(column * slabs_dev, slabs_dev)
    gathers = []
    for d in range(1, inner):
        gathers.append(
            remote(weights.at[spot], weights.at[spot], ks.at[d - 1], kr.at[d - 1], row_peer(d))
        )
        gathers.append(
            remote(field.at[block], field.at[block], gs.at[d - 1], gr.at[d - 1], row_peer(d))
        )
    for copy in gathers:
        copy.start()

    wi = lax.broadcasted_iota(jnp.int32, (width, width), 0)
    wj = lax.broadcasted_iota(jnp.int32, (width, width), 1)
    near = jnp.where((wi == wj + 1) | (wj == wi + 1), 1.0, 0.0)
    same = jnp.where(wi == wj, 1.0, 0.0)
    flip = jnp.where(wi + wj == width - 1, 1.0, 0.0)
    across = (2.0 * same - near).astype(jnp.bfloat16)
    opposite = (same - flip).astype(jnp.bfloat16)
    ri = lax.broadcasted_iota(jnp.int32, (local, rows), 0)
    rj = lax.broadcasted_iota(jnp.int32, (local, rows), 1)
    source = ri + column * own
    for a in range(1, outer):
        source = source + jnp.where(ri >= a * own, inner * own - own, 0)
    select = jnp.where(rj == source, 1.0, 0.0).astype(jnp.bfloat16)
    lvl[...] = jnp.zeros_like(lvl)

    for copy in gathers:
        copy.wait()
    halos = [
        remote(field.at[slabs], field.at[0], hs.at[0], hr.at[0], col_peer(1)),
        remote(field.at[1], field.at[slabs + 1], hs.at[1], hr.at[1], col_peer(outer - 1)),
    ]
    for copy in halos:
        copy.start()
    for copy in halos:
        copy.wait()

    @pl.loop(0, slabs + 2)
    def _(s):
        mine[s] = jnp.dot(select, field[s], preferred_element_type=jnp.float32).astype(
            jnp.bfloat16
        )

    @pl.loop(0, inner)
    def _(b):
        for s in range(slabs_dev):
            at = b * slabs_dev + s
            for term in range(terms):
                value = one_action(
                    term,
                    mine[at + 1],
                    mine[at],
                    mine[at + 2],
                    across,
                    opposite,
                    weights[at, term : term + 1, :],
                )
                lhs[b, term * local : (term + 1) * local, s * width : (s + 1) * width] = value
                wide = value.astype(jnp.float32)
                lvl[term : term + 1, :] += jnp.sum(wide * wide, axis=0, keepdims=True)

    cols = [
        remote(lvl, lvl_col.at[d - 1], cs.at[d - 1], cr.at[d - 1], col_peer(d))
        for d in range(1, outer)
    ]
    for copy in cols:
        copy.start()

    sends = []
    rowsends = []
    for turn, second in enumerate(reversed(range(terms))):
        deep = (second + 1) * local
        acc[0:deep, :] = jnp.zeros((deep, rows), jnp.float32)

        @pl.loop(0, inner)
        def _(b, second=second, deep=deep):
            for s in range(slabs_dev):
                at = b * slabs_dev + s
                act[:, s * width : (s + 1) * width] = one_action(
                    second,
                    field[at + 1],
                    field[at],
                    field[at + 2],
                    across,
                    opposite,
                    weights[at, second : second + 1, :],
                )
            acc[0:deep, :] += lax.dot_general(
                lhs[b, 0:deep, :],
                act[...],
                (((1,), (1,)), ((), ())),
                preferred_element_type=jnp.float32,
            )

        for a in range(outer):
            for first in range(second + 1):
                stages[second][a, first * own : (first + 1) * own, :] = acc[
                    first * local + a * own : first * local + (a + 1) * own, :
                ]
        for d in range(1, outer):
            n = second * (outer - 1) + d - 1
            copy = remote(
                stages[second].at[lax.rem(plane + d, outer)],
                arrived[second].at[d - 1],
                zs.at[n],
                zr.at[n],
                col_peer(d),
            )
            copy.start()
            sends.append((second, copy))
        if turn == 0:
            for copy in cols:
                copy.wait()
            mid = lvl[...]
            for d in range(1, outer):
                mid = mid + lvl_col[d - 1]
            lvl_mid[...] = mid
            rowsends = [
                remote(lvl_mid, lvl_row.at[d - 1], rs.at[d - 1], rr.at[d - 1], row_peer(d))
                for d in range(1, inner)
            ]
            for copy in rowsends:
                copy.start()

    for copy in rowsends:
        copy.wait()
    total = lvl_mid[...]
    for d in range(1, inner):
        total = total + lvl_row[d - 1]
    level = jnp.sum(total, axis=1, keepdims=True) / (rows * total_cells) + 1e-06
    for second in reversed(range(terms)):
        for q, copy in sends:
            if q == second:
                copy.wait()
        for first in range(second + 1):
            part = pl.ds(first * own, own)
            value = stages[second][plane, part, :]
            for d in range(1, outer):
                value = value + arrived[second][d - 1, part, :]
            factor = 1.0 / (
                total_cells * jnp.sqrt(level[first : first + 1] * level[second : second + 1])
            )
            pair = first * terms - first * (first - 1) // 2 + second - first
            out[pair] = value * factor


def per_device(basis, slab_region, coef_index, coef_table):
    terms = coef_index.shape[1]
    rows, cells_dev = basis.shape
    slabs_dev = slab_region.shape[0]
    width = cells_dev // slabs_dev
    devices = lax.axis_size("mode")
    inner = plane_size(devices, 2 * terms * rows * cells_dev)
    outer = devices // inner
    own = rows // devices
    slabs = slabs_dev * inner
    local = outer * own
    slab_kappa = slab_weights(slab_region, coef_index, coef_table)
    kap = jnp.broadcast_to(
        jnp.pad(slab_kappa, ((0, 0), (0, -terms % 8)))[:, :, None],
        (slabs_dev, terms + -terms % 8, width),
    )
    tall = terms + -terms % 8
    f32, b16 = jnp.float32, jnp.bfloat16
    deep = [(q + 1) * own for q in range(terms)]
    dma = pltpu.SemaphoreType.DMA
    return pl.pallas_call(
        functools.partial(
            gram_kernel, terms, inner, outer, own, slabs_dev, cells_dev * devices
        ),
        out_shape=jax.ShapeDtypeStruct((terms * (terms + 1) // 2, own, rows), f32),
        in_specs=[pl.BlockSpec(memory_space=pl.ANY)] * 2,
        out_specs=pl.BlockSpec(memory_space=pltpu.VMEM),
        scratch_shapes=[
            pltpu.VMEM((slabs + 2, rows, width), b16),
            pltpu.VMEM((slabs, tall, width), f32),
            pltpu.VMEM((slabs + 2, local, width), b16),
            pltpu.VMEM((inner, terms * local, cells_dev), b16),
            pltpu.VMEM((rows, cells_dev), b16),
            pltpu.VMEM((terms * local, rows), f32),
        ]
        + [pltpu.VMEM((outer, n, rows), f32) for n in deep]
        + [pltpu.VMEM((outer - 1, n, rows), f32) for n in deep]
        + [
            pltpu.VMEM((tall, width), f32),
            pltpu.VMEM((outer - 1, tall, width), f32),
            pltpu.VMEM((tall, width), f32),
            pltpu.VMEM((inner - 1, tall, width), f32),
            dma((slabs_dev + 1,)),
            dma((inner - 1,)),
            dma((inner - 1,)),
            dma((inner - 1,)),
            dma((inner - 1,)),
            dma((2,)),
            dma((2,)),
            dma((terms * (outer - 1),)),
            dma((terms * (outer - 1),)),
            dma((outer - 1,)),
            dma((outer - 1,)),
            dma((inner - 1,)),
            dma((inner - 1,)),
        ],
        compiler_params=pltpu.CompilerParams(
            collective_id=0, has_side_effects=True, vmem_limit_bytes=48 << 20
        ),
    )(basis, kap)


def solution(mesh):
    return jax.shard_map(
        per_device,
        mesh=mesh,
        in_specs=(P("groups", "mode"), P(("groups", "mode")), P("groups", None), P("groups")),
        out_specs=P(None, ("groups", "mode"), None),
        check_vma=False,
    )
```

time: 348 us -> 99.3 us (0.29)
  local copies, waits for them, and re-layouts: 164 us -> 2.07 us
  Pallas kernels: 0 us -> 95.4 us
  other arithmetic: 45.6 us -> 1.59 us
  between operations: 43 us -> 0.02 us
  blocking collectives: 39.4 us -> 0 us
  waiting for transfers between devices: 34.8 us -> 0 us
  matrix products: 15.6 us -> 0 us
  starting transfers between devices: 3.87 us -> 0 us
    convert_element_type x16 -> x0, local copies, waits for them, and re-layouts: 95.6 us -> none  [the longest x8 38.3 us: term_actions(): return [(slab_kappa[None, :, term, None] * stencils[term]).reshape(rows,...]
    pallas_call x0 -> x1, Pallas kernels: none -> 95.4 us  [per_device(): pl.pallas_call(functools.partial(gram_kernel, terms, inner, outer, own, s...]
    psum x1 -> x0, blocking collectives: 39.4 us -> none  [per_device(): lax.psum(jnp.stack([jnp.sum(jnp.square(v.astype(jnp.float32))) for v in m...]
    all_gather x1 -> x0, waiting for transfers between devices: 34.7 us -> none  [per_device(): lax.all_gather(jnp.concatenate([basis, tags], axis=0), 'mode', axis_index...]
    convert_element_type x6 -> x0, other arithmetic: 33.8 us -> none  [the longest x2 20.1 us: term_actions(): return [(slab_kappa[None, :, term, None] * stencils[term]).reshape(rows,...]
    rev x1 -> x0, local copies, waits for them, and re-layouts: 31.4 us -> none  [term_actions(): mirror = field[:, :, ::-1]]
    dot_general x21 -> x0, matrix products: 15.6 us -> none  [per_device(): lax.dot_general(mine[first], acts[second], (((1,), (1,)), ((), ())), pref...]
    slice x6 -> x0, local copies, waits for them, and re-layouts: 14.2 us -> none  [the longest x1 5.62 us: term_actions(): left_w = jnp.concatenate([zero_col, field[:, :, :-1]], axis=2)]
  transfers between devices with their start and end apart: 4 -> 0, of which waited for: 1 -> 0; matrix products, arithmetic and copies ran while one was open for 19% -> 0% of each run, Pallas kernels for 0% -> 0%
where the time goes in v2:
time: 99.3 us; the launch traced here: 99.1 us
  Pallas kernels  95.4 us (96%)
  local copies, waits for them, and re-layouts  2.07 us (2%)
  other arithmetic  1.59 us (2%)
    pallas_call x1, Pallas kernels, per_device(): pl.pallas_call(functools.partial(gram_kernel, terms, inner, outer, own, s...  95.4 us

profile of v2, /device:TPU:0, one launch (start us, length us, event | category | flops | bytes accessed | tf_op | source)
XLA Modules:
  0.0 99.1 jit_solution(6041518941243384883)
XLA Ops:
  0.0 0.0 copy-start.1
  0.0 0.7 fusion
  0.7 0.0 copy-done.1
  0.7 0.8 select_reduce_fusion
  1.5 0.1 multiply_reduce_fusion
  1.6 0.1 copy.9
  1.7 0.1 broadcast_in_dim.2.refs_1_
  1.8 0.0 copy-start
  1.8 1.0 %copy-done = bf16[384,512]{1,0:T(8,128)(2,1)S(1)} copy-done((bf16[384,512]{1,0:T(8,128)(2,1)S(1)}, bf16[384,512]{1,0:T(8,128)(2,1)}, u32[]{:S(2)}) %copy-start) | copy-done | bytes 393240
  2.8 95.4 %shard_map.46 = f32[21,12,384]{2,1,0:T(8,128)S(1)} custom-call(bf16[384,512]{1,0:T(8,128)(2,1)S(1)} %copy-done, f32[4,8,128]{2,1,0:T(8,128)S(1)} %broadcast_in_dim.2.refs_1_), custom_call_target="tpu_custom_call" | custom-call | tf_op jit(solution)/shard_map/pallas_call | solution.py:280
  98.2 0.9 copy.8
  (1 shorter events, 0.0 us)
Async XLA Ops:
  0.0 0.7 copy-start.1
  1.8 1.0 %copy-start = (bf16[384,512]{1,0:T(8,128)(2,1)S(1)}, bf16[384,512]{1,0:T(8,128)(2,1)}, u32[]{:S(2)}) copy-start(bf16[384,512]{1,0:T(8,128)(2,1)} %refs_0_.1) | copy-start | bytes 1179652

commit v3 on v2

--- a/solution.py
+++ b/solution.py
@@ -109,17 +109,26 @@
     for copy in loads:
         copy.wait()
 
-    block = pl.ds(1 + column * slabs_dev, slabs_dev)
+    chips = inner // 2
+    chip = column // 2
+    core = column % 2
+    sibling = plane * inner + chip * 2 + 1 - core
     spot = pl.ds(column * slabs_dev, slabs_dev)
-    gathers = []
-    for d in range(1, inner):
-        gathers.append(
-            remote(weights.at[spot], weights.at[spot], ks.at[d - 1], kr.at[d - 1], row_peer(d))
-        )
-        gathers.append(
-            remote(field.at[block], field.at[block], gs.at[d - 1], gr.at[d - 1], row_peer(d))
-        )
-    for copy in gathers:
+    small = [
+        remote(weights.at[spot], weights.at[spot], ks.at[d - 1], kr.at[d - 1], row_peer(d))
+        for d in range(1, inner)
+    ]
+
+    def push(origin, slot, peer):
+        span = pl.ds(1 + origin * slabs_dev, slabs_dev)
+        return remote(field.at[span], field.at[span], gs.at[slot], gr.at[slot], peer)
+
+    far = [
+        push(column, d, plane * inner + lax.rem(chip + d, chips) * 2 + core)
+        for d in range(1, chips)
+    ]
+    gathers = [push(column, 0, sibling)]
+    for copy in small + far + gathers:
         copy.start()
 
     wi = lax.broadcasted_iota(jnp.int32, (width, width), 0)
@@ -137,7 +146,15 @@
     select = jnp.where(rj == source, 1.0, 0.0).astype(jnp.bfloat16)
     lvl[...] = jnp.zeros_like(lvl)
 
-    for copy in gathers:
+    for d, copy in enumerate(far, 1):
+        copy.wait_recv()
+        origin = lax.rem(chip + chips - d, chips) * 2 + core
+        relay = push(origin, chips - 1 + d, sibling)
+        relay.start()
+        gathers.append(relay)
+    for copy in far:
+        copy.wait_send()
+    for copy in small + gathers:
         copy.wait()
     halos = [
         remote(field.at[slabs], field.at[0], hs.at[0], hr.at[0], col_peer(1)),

time: 99.3 us -> 85.1 us (0.86)
  Pallas kernels: 95.4 us -> 81.2 us
    pallas_call x1, Pallas kernels: 95.4 us -> 81.2 us  [per_device(): pl.pallas_call(functools.partial(gram_kernel, terms, inner, outer, own, s...]
where the time goes in v3:
time: 85.1 us; the launch traced here: 84.9 us
  Pallas kernels  81.2 us (95%)
  local copies, waits for them, and re-layouts  2.07 us (2%)
  other arithmetic  1.59 us (2%)
    pallas_call x1, Pallas kernels, per_device(): pl.pallas_call(functools.partial(gram_kernel, terms, inner, outer, own, s...  81.2 us

profile of v3, /device:TPU:0, one launch (start us, length us, event | category | flops | bytes accessed | tf_op | source)
XLA Modules:
  0.0 84.9 jit_solution(8483403193582135064)
XLA Ops:
  0.0 0.0 copy-start.1
  0.0 0.7 fusion
  0.7 0.0 copy-done.1
  0.7 0.8 select_reduce_fusion
  1.5 0.1 multiply_reduce_fusion
  1.6 0.1 copy.9
  1.7 0.1 broadcast_in_dim.2.refs_1_
  1.8 0.0 copy-start
  1.8 1.0 %copy-done = bf16[384,512]{1,0:T(8,128)(2,1)S(1)} copy-done((bf16[384,512]{1,0:T(8,128)(2,1)S(1)}, bf16[384,512]{1,0:T(8,128)(2,1)}, u32[]{:S(2)}) %copy-start) | copy-done | bytes 393240
  2.8 81.2 %shard_map.46 = f32[21,12,384]{2,1,0:T(8,128)S(1)} custom-call(bf16[384,512]{1,0:T(8,128)(2,1)S(1)} %copy-done, f32[4,8,128]{2,1,0:T(8,128)S(1)} %broadcast_in_dim.2.refs_1_), custom_call_target="tpu_custom_call" | custom-call | tf_op jit(solution)/shard_map/pallas_call | solution.py:297
  84.0 0.9 %copy.8 = f32[21,12,384]{2,0,1:T(8,128)} copy(f32[21,12,384]{2,1,0:T(8,128)S(1)} %shard_map.46) | data formatting | bytes 774144 | tf_op jit(solution)/shard_map/pallas_call | solution.py:297
  (1 shorter events, 0.0 us)
Async XLA Ops:
  0.0 0.7 copy-start.1
  1.8 1.0 %copy-start = (bf16[384,512]{1,0:T(8,128)(2,1)S(1)}, bf16[384,512]{1,0:T(8,128)(2,1)}, u32[]{:S(2)}) copy-start(bf16[384,512]{1,0:T(8,128)(2,1)} %refs_0_.1) | copy-start | bytes 1179652

commit v4 on v3

--- a/solution.py
+++ b/solution.py
@@ -146,15 +146,53 @@
     select = jnp.where(rj == source, 1.0, 0.0).astype(jnp.bfloat16)
     lvl[...] = jnp.zeros_like(lvl)
 
+    def pick(first, count):
+        for s in range(count):
+            mine[first + s] = jnp.dot(
+                select, field[first + s], preferred_element_type=jnp.float32
+            ).astype(jnp.bfloat16)
+
+    def own_actions(b, chosen):
+        for term in chosen:
+            squares = None
+            for s in range(slabs_dev):
+                at = b * slabs_dev + s
+                value = one_action(
+                    term,
+                    mine[at + 1],
+                    None if term in alone else mine[at],
+                    None if term in alone else mine[at + 2],
+                    across,
+                    opposite,
+                    weights[at, term : term + 1, :],
+                )
+                lhs[b, term * local : (term + 1) * local, s * width : (s + 1) * width] = value
+                wide = value.astype(jnp.float32)
+                squares = wide * wide if squares is None else squares + wide * wide
+            lvl[term : term + 1, :] += jnp.sum(squares, axis=0, keepdims=True)
+
+    alone = (1, 4, 5)
+    coupled = tuple(term for term in range(terms) if term not in alone)
+
+    def settle(origin):
+        pick(1 + origin * slabs_dev, slabs_dev)
+        own_actions(origin, alone)
+
+    for copy in small:
+        copy.wait()
+    settle(column)
+    gathers[0].wait()
+    settle(chip * 2 + 1 - core)
     for d, copy in enumerate(far, 1):
         copy.wait_recv()
         origin = lax.rem(chip + chips - d, chips) * 2 + core
         relay = push(origin, chips - 1 + d, sibling)
         relay.start()
         gathers.append(relay)
+        settle(origin)
     for copy in far:
         copy.wait_send()
-    for copy in small + gathers:
+    for copy in gathers[1:]:
         copy.wait()
     halos = [
         remote(field.at[slabs], field.at[0], hs.at[0], hr.at[0], col_peer(1)),
@@ -162,32 +200,19 @@
     ]
     for copy in halos:
         copy.start()
+    for d in range(1, chips):
+        settle(lax.rem(chip + chips - d, chips) * 2 + 1 - core)
+
+    @pl.loop(1, inner - 1)
+    def _(b):
+        own_actions(b, coupled)
+
     for copy in halos:
         copy.wait()
-
-    @pl.loop(0, slabs + 2)
-    def _(s):
-        mine[s] = jnp.dot(select, field[s], preferred_element_type=jnp.float32).astype(
-            jnp.bfloat16
-        )
-
-    @pl.loop(0, inner)
-    def _(b):
-        for s in range(slabs_dev):
-            at = b * slabs_dev + s
-            for term in range(terms):
-                value = one_action(
-                    term,
-                    mine[at + 1],
-                    mine[at],
-                    mine[at + 2],
-                    across,
-                    opposite,
-                    weights[at, term : term + 1, :],
-                )
-                lhs[b, term * local : (term + 1) * local, s * width : (s + 1) * width] = value
-                wide = value.astype(jnp.float32)
-                lvl[term : term + 1, :] += jnp.sum(wide * wide, axis=0, keepdims=True)
+    pick(0, 1)
+    pick(slabs + 1, 1)
+    own_actions(0, coupled)
+    own_actions(inner - 1, coupled)
 
     cols = [
         remote(lvl, lvl_col.at[d - 1], cs.at[d - 1], cr.at[d - 1], col_peer(d))

time: 85.1 us -> 78.5 us (0.922)
  Pallas kernels: 81.2 us -> 74.6 us
    pallas_call x1, Pallas kernels: 81.2 us -> 74.6 us  [per_device(): pl.pallas_call(functools.partial(gram_kernel, terms, inner, outer, own, s...]
where the time goes in v4:
time: 78.5 us; the launch traced here: 78.3 us
  Pallas kernels  74.6 us (95%)
  local copies, waits for them, and re-layouts  2.07 us (3%)
  other arithmetic  1.59 us (2%)
    pallas_call x1, Pallas kernels, per_device(): pl.pallas_call(functools.partial(gram_kernel, terms, inner, outer, own, s...  74.6 us

profile of v4, /device:TPU:0, one launch (start us, length us, event | category | flops | bytes accessed | tf_op | source)
XLA Modules:
  0.0 78.3 jit_solution(16628226708164508643)
XLA Ops:
  0.0 0.0 copy-start.1
  0.0 0.7 fusion
  0.7 0.0 copy-done.1
  0.7 0.8 select_reduce_fusion
  1.5 0.1 multiply_reduce_fusion
  1.6 0.1 copy.9
  1.7 0.1 broadcast_in_dim.2.refs_1_
  1.8 0.0 copy-start
  1.8 1.0 %copy-done = bf16[384,512]{1,0:T(8,128)(2,1)S(1)} copy-done((bf16[384,512]{1,0:T(8,128)(2,1)S(1)}, bf16[384,512]{1,0:T(8,128)(2,1)}, u32[]{:S(2)}) %copy-start) | copy-done | bytes 393240
  2.8 74.6 %shard_map.46 = f32[21,12,384]{2,1,0:T(8,128)S(1)} custom-call(bf16[384,512]{1,0:T(8,128)(2,1)S(1)} %copy-done, f32[4,8,128]{2,1,0:T(8,128)S(1)} %broadcast_in_dim.2.refs_1_), custom_call_target="tpu_custom_call" | custom-call | tf_op jit(solution)/shard_map/pallas_call | solution.py:322
  77.4 0.9 %copy.8 = f32[21,12,384]{2,0,1:T(8,128)} copy(f32[21,12,384]{2,1,0:T(8,128)S(1)} %shard_map.46) | data formatting | bytes 774144 | tf_op jit(solution)/shard_map/pallas_call | solution.py:322
  (1 shorter events, 0.0 us)
Async XLA Ops:
  0.0 0.7 copy-start.1
  1.8 1.0 %copy-start = (bf16[384,512]{1,0:T(8,128)(2,1)S(1)}, bf16[384,512]{1,0:T(8,128)(2,1)}, u32[]{:S(2)}) copy-start(bf16[384,512]{1,0:T(8,128)(2,1)} %refs_0_.1) | copy-start | bytes 1179652

commit v5 on v4

--- a/solution.py
+++ b/solution.py
@@ -54,8 +54,11 @@
     field, weights, mine, lhs, act, acc = refs[3:9]
     stages = refs[9 : 9 + terms]
     arrived = refs[9 + terms : 9 + 2 * terms]
-    lvl, lvl_col, lvl_mid, lvl_row = refs[9 + 2 * terms : 13 + 2 * terms]
-    load_sem, gs, gr, ks, kr, hs, hr, zs, zr, cs, cr, rs, rr = refs[13 + 2 * terms :]
+    codes = refs[9 + 2 * terms : 9 + 3 * terms]
+    scales = refs[9 + 3 * terms : 9 + 4 * terms]
+    got_scales = refs[9 + 4 * terms : 9 + 5 * terms]
+    lvl, lvl_col, lvl_mid, lvl_row, whole, ss, sr = refs[9 + 5 * terms : 16 + 5 * terms]
+    load_sem, gs, gr, ks, kr, hs, hr, zs, zr, cs, cr, rs, rr = refs[16 + 5 * terms :]
     rows, width = field.shape[1], field.shape[2]
     slabs = inner * slabs_dev
     local = outer * own
@@ -249,13 +252,31 @@
 
         for a in range(outer):
             for first in range(second + 1):
-                stages[second][a, first * own : (first + 1) * own, :] = acc[
-                    first * local + a * own : first * local + (a + 1) * own, :
-                ]
+                value = acc[first * local + a * own : first * local + (a + 1) * own, :]
+                stages[second][a, first * own : (first + 1) * own, :] = value
+                peak = jnp.max(jnp.abs(value), axis=0, keepdims=True)
+                scale = peak * (1.0 / 32000.0)
+                scale = jnp.where(scale > 0.0, scale, 1.0)
+                scales[second][a, first : first + 1, :] = scale
+                whole[first * own : (first + 1) * own, :] = jnp.round(
+                    jnp.clip(value / scale, -32767.0, 32767.0)
+                )
+            codes[second][a] = (
+                whole[0 : (second + 1) * own, :].astype(jnp.int32).astype(jnp.int16)
+            )
         for d in range(1, outer):
             n = second * (outer - 1) + d - 1
+            scale_copy = remote(
+                scales[second].at[lax.rem(plane + d, outer)],
+                got_scales[second].at[d - 1],
+                ss.at[n],
+                sr.at[n],
+                col_peer(d),
+            )
+            scale_copy.start()
+            sends.append((second, scale_copy))
             copy = remote(
-                stages[second].at[lax.rem(plane + d, outer)],
+                codes[second].at[lax.rem(plane + d, outer)],
                 arrived[second].at[d - 1],
                 zs.at[n],
                 zr.at[n],
@@ -287,11 +308,18 @@
         for q, copy in sends:
             if q == second:
                 copy.wait()
+        opened = [
+            arrived[second][d - 1].astype(jnp.int32).astype(jnp.float32)
+            for d in range(1, outer)
+        ]
         for first in range(second + 1):
             part = pl.ds(first * own, own)
             value = stages[second][plane, part, :]
             for d in range(1, outer):
-                value = value + arrived[second][d - 1, part, :]
+                value = value + (
+                    opened[d - 1][first * own : (first + 1) * own, :]
+                    * got_scales[second][d - 1, first : first + 1, :]
+                )
             factor = 1.0 / (
                 total_cells * jnp.sqrt(level[first : first + 1] * level[second : second + 1])
             )
@@ -335,12 +363,18 @@
             pltpu.VMEM((terms * local, rows), f32),
         ]
         + [pltpu.VMEM((outer, n, rows), f32) for n in deep]
-        + [pltpu.VMEM((outer - 1, n, rows), f32) for n in deep]
+        + [pltpu.VMEM((outer - 1, n, rows), jnp.int16) for n in deep]
+        + [pltpu.VMEM((outer, n, rows), jnp.int16) for n in deep]
+        + [pltpu.VMEM((outer, n + 1, rows), f32) for n in range(terms)]
+        + [pltpu.VMEM((outer - 1, n + 1, rows), f32) for n in range(terms)]
         + [
             pltpu.VMEM((tall, width), f32),
             pltpu.VMEM((outer - 1, tall, width), f32),
             pltpu.VMEM((tall, width), f32),
             pltpu.VMEM((inner - 1, tall, width), f32),
+            pltpu.VMEM((deep[-1], rows), f32),
+            dma((terms * (outer - 1),)),
+            dma((terms * (outer - 1),)),
             dma((slabs_dev + 1,)),
             dma((inner - 1,)),
             dma((inner - 1,)),

time: 78.5 us -> 65.3 us (0.83)
  Pallas kernels: 74.6 us -> 61.5 us
    pallas_call x1, Pallas kernels: 74.6 us -> 61.5 us  [per_device(): pl.pallas_call(functools.partial(gram_kernel, terms, inner, outer, own, s...]
where the time goes in v5:
time: 65.3 us; the launch traced here: 65.1 us
  Pallas kernels  61.5 us (94%)
  local copies, waits for them, and re-layouts  2.07 us (3%)
  other arithmetic  1.59 us (2%)
    pallas_call x1, Pallas kernels, per_device(): pl.pallas_call(functools.partial(gram_kernel, terms, inner, outer, own, s...  61.5 us

profile of v5, /device:TPU:0, one launch (start us, length us, event | category | flops | bytes accessed | tf_op | source)
XLA Modules:
  0.0 65.1 jit_solution(2879453854459321024)
XLA Ops:
  0.0 0.0 copy-start.1
  0.0 0.7 %fusion = f32[4,9]{1,0:T(4,128)S(1)} fusion(s32[4]{0:T(128)} %param.5), kind=kLoop, calls=%fused_computation.4 | loop fusion | flops 72 | bytes 160 | tf_op jit(solution)/shard_map/convert_element_type | solution.py:29
  0.7 0.0 copy-done.1
  0.7 0.8 %select_reduce_fusion = f32[9,6]{0,1:T(8,128)S(1)} fusion(f32[8]{0:T(128)S(1)} %copy-done.1, s32[9,6]{0,1:T(8,128)} %param.6), kind=kLoop, calls=%fused_computation | loop fusion | flops 1242 | bytes 464 | tf_op jit(solution)/shard_map/reduce_sum | solution.py:28
  1.5 0.1 multiply_reduce_fusion
  1.6 0.1 copy.9
  1.7 0.1 broadcast_in_dim.2.refs_1_
  1.8 0.0 copy-start
  1.8 1.0 %copy-done = bf16[384,512]{1,0:T(8,128)(2,1)S(1)} copy-done((bf16[384,512]{1,0:T(8,128)(2,1)S(1)}, bf16[384,512]{1,0:T(8,128)(2,1)}, u32[]{:S(2)}) %copy-start) | copy-done | bytes 393240
  2.8 61.5 %shard_map.46 = f32[21,12,384]{2,1,0:T(8,128)S(1)} custom-call(bf16[384,512]{1,0:T(8,128)(2,1)S(1)} %copy-done, f32[4,8,128]{2,1,0:T(8,128)S(1)} %broadcast_in_dim.2.refs_1_), custom_call_target="tpu_custom_call" | custom-call | tf_op jit(solution)/shard_map/pallas_call | solution.py:350
  64.2 0.9 %copy.8 = f32[21,12,384]{2,0,1:T(8,128)} copy(f32[21,12,384]{2,1,0:T(8,128)S(1)} %shard_map.46) | data formatting | bytes 774144 | tf_op jit(solution)/shard_map/pallas_call | solution.py:350
  (1 shorter events, 0.0 us)
Async XLA Ops:
  0.0 0.7 %copy-start.1 = (f32[8]{0:T(128)S(1)}, f32[8]{0:T(128)}, u32[]{:S(2)}) copy-start(f32[8]{0:T(128)} %param.7) | copy-start | bytes 100
  1.8 1.0 %copy-start = (bf16[384,512]{1,0:T(8,128)(2,1)S(1)}, bf16[384,512]{1,0:T(8,128)(2,1)}, u32[]{:S(2)}) copy-start(bf16[384,512]{1,0:T(8,128)(2,1)} %refs_0_.1) | copy-start | bytes 1179652

commit v6 on v5

--- a/solution.py
+++ b/solution.py
@@ -230,25 +230,30 @@
         deep = (second + 1) * local
         acc[0:deep, :] = jnp.zeros((deep, rows), jnp.float32)
 
-        @pl.loop(0, inner)
-        def _(b, second=second, deep=deep):
-            for s in range(slabs_dev):
-                at = b * slabs_dev + s
-                act[:, s * width : (s + 1) * width] = one_action(
-                    second,
-                    field[at + 1],
-                    field[at],
-                    field[at + 2],
-                    across,
-                    opposite,
-                    weights[at, second : second + 1, :],
+        @pl.loop(0, inner // 2)
+        def _(half, second=second, deep=deep):
+            for u in range(2):
+                for s in range(slabs_dev):
+                    at = (half * 2 + u) * slabs_dev + s
+                    act[u, :, s * width : (s + 1) * width] = one_action(
+                        second,
+                        field[at + 1],
+                        field[at],
+                        field[at + 2],
+                        across,
+                        opposite,
+                        weights[at, second : second + 1, :],
+                    )
+            sums = [
+                lax.dot_general(
+                    lhs[half * 2 + u, 0:deep, :],
+                    act[u],
+                    (((1,), (1,)), ((), ())),
+                    preferred_element_type=jnp.float32,
                 )
-            acc[0:deep, :] += lax.dot_general(
-                lhs[b, 0:deep, :],
-                act[...],
-                (((1,), (1,)), ((), ())),
-                preferred_element_type=jnp.float32,
-            )
+                for u in range(2)
+            ]
+            acc[0:deep, :] += sums[0] + sums[1]
 
         for a in range(outer):
             for first in range(second + 1):
@@ -359,7 +364,7 @@
             pltpu.VMEM((slabs, tall, width), f32),
             pltpu.VMEM((slabs + 2, local, width), b16),
             pltpu.VMEM((inner, terms * local, cells_dev), b16),
-            pltpu.VMEM((rows, cells_dev), b16),
+            pltpu.VMEM((2, rows, cells_dev), b16),
             pltpu.VMEM((terms * local, rows), f32),
         ]
         + [pltpu.VMEM((outer, n, rows), f32) for n in deep]

time: 65.3 us -> 64.5 us (0.988)
  Pallas kernels: 61.5 us -> 60.6 us
    pallas_call x1, Pallas kernels: 61.5 us -> 60.6 us  [per_device(): pl.pallas_call(functools.partial(gram_kernel, terms, inner, outer, own, s...]
where the time goes in v6:
time: 64.5 us; the launch traced here: 64.3 us
  Pallas kernels  60.6 us (94%)
  local copies, waits for them, and re-layouts  2.07 us (3%)
  other arithmetic  1.59 us (2%)
    pallas_call x1, Pallas kernels, per_device(): pl.pallas_call(functools.partial(gram_kernel, terms, inner, outer, own, s...  60.6 us

profile of v6, /device:TPU:0, one launch (start us, length us, event | category | flops | bytes accessed | tf_op | source)
XLA Modules:
  0.0 64.3 jit_solution(15389119947024823515)
XLA Ops:
  0.0 0.0 copy-start.1
  0.0 0.7 %fusion = f32[4,9]{1,0:T(4,128)S(1)} fusion(s32[4]{0:T(128)} %param.5), kind=kLoop, calls=%fused_computation.4 | loop fusion | flops 72 | bytes 160 | tf_op jit(solution)/shard_map/convert_element_type | solution.py:29
  0.7 0.0 copy-done.1
  0.7 0.8 %select_reduce_fusion = f32[9,6]{0,1:T(8,128)S(1)} fusion(f32[8]{0:T(128)S(1)} %copy-done.1, s32[9,6]{0,1:T(8,128)} %param.6), kind=kLoop, calls=%fused_computation | loop fusion | flops 1242 | bytes 464 | tf_op jit(solution)/shard_map/reduce_sum | solution.py:28
  1.5 0.1 multiply_reduce_fusion
  1.6 0.1 copy.9
  1.7 0.1 broadcast_in_dim.2.refs_1_
  1.8 0.0 copy-start
  1.8 1.0 %copy-done = bf16[384,512]{1,0:T(8,128)(2,1)S(1)} copy-done((bf16[384,512]{1,0:T(8,128)(2,1)S(1)}, bf16[384,512]{1,0:T(8,128)(2,1)}, u32[]{:S(2)}) %copy-start) | copy-done | bytes 393240
  2.8 60.6 %shard_map.46 = f32[21,12,384]{2,1,0:T(8,128)S(1)} custom-call(bf16[384,512]{1,0:T(8,128)(2,1)S(1)} %copy-done, f32[4,8,128]{2,1,0:T(8,128)S(1)} %broadcast_in_dim.2.refs_1_), custom_call_target="tpu_custom_call" | custom-call | tf_op jit(solution)/shard_map/pallas_call | solution.py:355
  63.4 0.9 %copy.8 = f32[21,12,384]{2,0,1:T(8,128)} copy(f32[21,12,384]{2,1,0:T(8,128)S(1)} %shard_map.46) | data formatting | bytes 774144 | tf_op jit(solution)/shard_map/pallas_call | solution.py:355
  (1 shorter events, 0.0 us)
Async XLA Ops:
  0.0 0.7 %copy-start.1 = (f32[8]{0:T(128)S(1)}, f32[8]{0:T(128)}, u32[]{:S(2)}) copy-start(f32[8]{0:T(128)} %param.7) | copy-start | bytes 100
  1.8 1.0 %copy-start = (bf16[384,512]{1,0:T(8,128)(2,1)S(1)}, bf16[384,512]{1,0:T(8,128)(2,1)}, u32[]{:S(2)}) copy-start(bf16[384,512]{1,0:T(8,128)(2,1)} %refs_0_.1) | copy-start | bytes 1179652
